TPU v7x, 512 devices: a whole 4x4x16 slice. The times are simulated.
512 devices in a mesh: cells: 32 (over z, core), genes: 16 (over x, y).
Axes of the slice: x: 4, y: 4, z: 16, core: 2. Of those that a mesh axis runs over, the one named last changes fastest.
Arguments:
- sketch: bfloat16 [32768, 256], P('cells'), may hold values from -6 to 6
- tiles: bfloat16 [49152, 128, 128], P(('cells', 'genes')), may hold values from -0.0546875 to 0.0546875
- tile_rows: int32 [49152], P(('cells', 'genes')), may hold values from 0 to 7, as said below
- tile_cols: int32 [49152], P(('cells', 'genes')), may hold values from 0 to 15
- tile_counts: int32 [512], P(('cells', 'genes')), may hold values from 16 to 96, as said below
Outputs:
- projected: float32 [32768, 256], P(('cells', 'genes'))
Inputs may be any that keep to these rules, and one draw needn't show every extreme that they name: Within one device's slots the pairs (tile_rows, tile_cols) are distinct. `tile_counts`: some device holds 96 tiles and the device half the cells axis away from it holds 16.
All inputs are finite; a program needn't handle non-finite values.
Results may differ from a plain program's by a relative error of at most 0.0021.
Values may be sent and summed in bfloat16 or wider, within the bound.
A program may use at most 128 MiB of HBM per device.

v0:
```python
import jax
import jax.numpy as jnp
from jax import lax
from jax.sharding import PartitionSpec as P

GENE_BLOCKS = 16


def selector(index_ids, slot_live, width):
    hits = (index_ids[:, None] == jnp.arange(width, dtype=jnp.int32)[None, :]).astype(jnp.float32)
    return hits * slot_live[:, None]


def local(sketch, tiles, tile_rows, tile_cols, tile_counts):
    tile_size = tiles.shape[1]
    sketch_width = sketch.shape[1]
    slot_total = tiles.shape[0]
    row_blocks = sketch.shape[0] // tile_size
    sketch_blocks = sketch.reshape(row_blocks, tile_size, sketch_width)
    slot_live = (jnp.arange(slot_total, dtype=jnp.int32) < tile_counts[0]).astype(jnp.float32)
    col_select = selector(tile_cols, slot_live, GENE_BLOCKS)
    row_select = selector(tile_rows, slot_live, row_blocks)
    picked_rows = sketch_blocks[tile_rows]
    first_terms = jnp.einsum("ski,skr->sir", tiles, picked_rows, preferred_element_type=jnp.float32)
    gene_acc = jnp.einsum("sg,sir->gir", col_select, first_terms, precision=lax.Precision.HIGHEST)
    gene_cast = lax.psum(gene_acc, "cells").astype(jnp.bfloat16)
    picked_genes = gene_cast[tile_cols]
    second_terms = jnp.einsum(
        "sik,skr->sir", tiles, picked_genes, preferred_element_type=jnp.float32
    )
    cell_acc = jnp.einsum("sb,sir->bir", row_select, second_terms, precision=lax.Precision.HIGHEST)
    return lax.psum_scatter(
        cell_acc.reshape(row_blocks * tile_size, sketch_width),
        "genes",
        scatter_dimension=0,
        tiled=True,
    )


def solution(mesh):
    in_specs = (
        P("cells", None),
        P(("cells", "genes"), None, None),
        P(("cells", "genes")),
        P(("cells", "genes")),
        P(("cells", "genes")),
    )
    out_specs = P(("cells", "genes"), None)
    return jax.shard_map(local, mesh=mesh, in_specs=in_specs, out_specs=out_specs, check_vma=False)
```

profile of v0, /device:TPU:2, one launch (start us, length us, event | category | flops | bytes accessed | tf_op | source)
XLA Modules:
  0.0 301.6 jit_solution(11839636375966423922)
XLA Ops:
  6.5 0.0 copy-start
  6.5 0.0 reduce-scatter.2.cloned.1.call-start
  7.4 0.8 compare_select_fusion.1
  8.2 7.0 %gather_fusion = bf16[96,128,256]{2,1,0:T(8,128)(2,1)} fusion(bf16[8,128,256]{2,1,0:T(8,128)(2,1)} %bitcast.20, s32[1024]{0:T(1024)S(1)} %pad_clamp_fusion.1), kind=kCustom, calls=%fused_computation | custom fusion | bytes 12583296 | tf_op jit(solution)/shard_map/gather | solution.py:23
  15.1 0.0 copy-done
  15.1 9.2 %convolution_bitcast_fusion = f32[96,128,256]{1,2,0:T(8,128)} fusion(bf16[96,128,256]{2,1,0:T(8,128)(2,1)} %gather_fusion, bf16[96,128,128]{2,1,0:T(8,128)(2,1)S(1)} %copy-done), kind=kOutput, calls=%fused_computation.4 | convolution fusion | flops 805306368 | bytes 22020096 | tf_op jit(solution)/shard_map/ski,skr->sir/dot_general | solution.py:24
  24.3 0.0 copy-start.1
  24.3 12.7 %copy.7 = f32[96,128,256]{2,0,1:T(8,128)} copy(f32[96,128,256]{1,2,0:T(8,128)} %convolution_bitcast_fusion) | data formatting | bytes 25165824 | tf_op jit(solution)/shard_map/ski,skr->sir/dot_general | solution.py:24
  37.0 0.0 copy-done.1
  37.0 9.1 %fusion.2 = f32[16,128,256]{2,0,1:T(8,128)S(1)} fusion(f32[96,128,256]{2,0,1:T(8,128)} %copy.7, f32[96]{0:T(128)S(1)} %compare_convert_fusion, s32[96]{0:T(128)S(1)} %copy-done.1), kind=kOutput, calls=%fused_computation.5 | convolution fusion | flops 603982848 | bytes 14680832 | tf_op jit(solution)/shard_map/sg,sir->gir/dot_general | solution.py:25
  46.1 2.6 copy.8
  48.7 122.1 %all-reduce.1 = bf16[16,128,256]{2,1,0:T(8,128)(2,1)} all-reduce(f32[16,128,256]{2,1,0:T(8,128)} %copy.8), channel_id=1, replica_groups=mesh['cells'=32,'genes'=16] {'cells'}, use_global_device_ids=true, to_apply=%region_0.0 | all-reduce | flops 524288 | bytes 3145728 | tf_op jit(solution)/shard_map/psum | solution.py:26
  170.8 7.2 %gather_fusion.1 = bf16[96,128,256]{2,1,0:T(8,128)(2,1)} fusion(bf16[16,128,256]{2,1,0:T(8,128)(2,1)} %all-reduce.1, s32[1024]{0:T(1024)S(1)} %pad_clamp_fusion), kind=kCustom, calls=%fused_computation.1 | custom fusion | bytes 12583296 | tf_op jit(solution)/shard_map/gather | solution.py:27
  177.9 9.2 %fusion.15 = f32[96,256,128]{2,1,0:T(8,128)} fusion(bf16[96,128,256]{2,1,0:T(8,128)(2,1)} %gather_fusion.1, bf16[96,128,128]{2,1,0:T(8,128)(2,1)S(1)} %copy-done), kind=kOutput, calls=%fused_computation.25 | convolution fusion | flops 805306368 | bytes 22020096 | tf_op jit(solution)/shard_map/sik,skr->sir/dot_general | solution.py:28
  187.1 0.0 copy-start.2
  187.1 12.7 %copy.9 = f32[96,256,128]{1,0,2:T(8,128)} copy(f32[96,256,128]{2,1,0:T(8,128)} %fusion.15) | data formatting | bytes 25165824 | tf_op jit(solution)/shard_map/sik,skr->sir/dot_general | solution.py:28
  199.8 0.0 copy-done.2
  199.8 8.9 %fusion = f32[8,128,256]{2,0,1:T(8,128)S(1)} fusion(f32[96,256,128]{1,0,2:T(8,128)} %copy.9, f32[96]{0:T(128)S(1)} %compare_convert_fusion, s32[96]{0:T(128)S(1)} %copy-done.2), kind=kOutput, calls=%fused_computation.2 | convolution fusion | flops 301991424 | bytes 13632256 | tf_op jit(solution)/shard_map/sb,sir->bir/dot_general | solution.py:31
  208.7 1.3 copy.6
  210.0 0.0 reduce-scatter.2.cloned.1.call-update
  210.1 84.7 %reduce-scatter.2.cloned.1.call-done = f32[64,256]{1,0:T(8,128)} async-done(((f32[1024,256]{1,0:T(8,128)}), f32[64,256]{1,0:T(8,128)}) %reduce-scatter.2.cloned.1.call-update) | async-done | bytes 65552 | tf_op jit(solution)/shard_map/reduce_scatter | solution.py:32
  (4 shorter events, 0.0 us)
Async XLA Ops:
  6.5 8.6 %copy-start = (bf16[96,128,128]{2,1,0:T(8,128)(2,1)S(1)}, bf16[96,128,128]{2,1,0:T(8,128)(2,1)}, u32[]{:S(2)}) copy-start(bf16[96,128,128]{2,1,0:T(8,128)(2,1)} %param.6) | copy-start | bytes 9437188
  6.5 288.2 %reduce-scatter.2.cloned.1.call-start = ((), (), s32[]{:S(2)}) async-start(), calls=%async_computation.1 | async-start | bytes 1114112 | tf_op jit(solution)/shard_map/reduce_scatter | solution.py:32
  24.3 12.7 %copy-start.1 = (s32[96]{0:T(128)S(1)}, s32[96]{0:T(128)}, u32[]{:S(2)}) copy-start(s32[96]{0:T(128)} %param.8) | copy-start | bytes 1156
  187.1 12.7 %copy-start.2 = (s32[96]{0:T(128)S(1)}, s32[96]{0:T(128)}, u32[]{:S(2)}) copy-start(s32[96]{0:T(128)} %param.7) | copy-start | bytes 1156
Sparse Core Ops, SparseCore 0:
  210.2 84.5 reduce-scatter.1
where the time goes:
time: 302 us
  blocking collectives  122 us (40%)
  waiting for transfers between devices  84.7 us (28%)
  local copies, waits for them, and re-layouts  43.4 us (14%)
  matrix products  36.3 us (12%)
  between operations  14.2 us (5%)
    psum x1, blocking collectives, local(): gene_cast = lax.psum(gene_acc, 'cells').astype(jnp.bfloat16)  122 us
    reduce_scatter x1, waiting for transfers between devices, local(): lax.psum_scatter(cell_acc.reshape(row_blocks * tile_size, sketch_width),...  84.7 us
    dot_general x1, local copies, waits for them, and re-layouts, local(): jnp.einsum('sik,skr->sir', tiles, picked_genes, preferred_element_type=jn...  12.7 us
    dot_general x1, local copies, waits for them, and re-layouts, local(): jnp.einsum('ski,skr->sir', tiles, picked_rows, preferred_element_type=jnp...  12.7 us
    dot_general x1, matrix products, local(): jnp.einsum('sik,skr->sir', tiles, picked_genes, preferred_element_type=jn...  9.19 us
    dot_general x1, matrix products, local(): jnp.einsum('ski,skr->sir', tiles, picked_rows, preferred_element_type=jnp...  9.19 us
    dot_general x1, matrix products, local(): jnp.einsum('sg,sir->gir', col_select, first_terms, precision=lax.Precisio...  9.05 us
    dot_general x1, matrix products, local(): jnp.einsum('sb,sir->bir', row_select, second_terms, precision=lax.Precisi...  8.9 us
  transfers between devices with their start and end apart: 1, of which 1 were waited for; matrix products, arithmetic and copies ran while one was open for 0% of the time, Pallas kernels for 0%

commit v1 on v0

--- a/solution.py
+++ b/solution.py
@@ -23,7 +23,7 @@
     picked_rows = sketch_blocks[tile_rows]
     first_terms = jnp.einsum("ski,skr->sir", tiles, picked_rows, preferred_element_type=jnp.float32)
     gene_acc = jnp.einsum("sg,sir->gir", col_select, first_terms, precision=lax.Precision.HIGHEST)
-    gene_cast = lax.psum(gene_acc, "cells").astype(jnp.bfloat16)
+    gene_cast = jnp.sum(lax.all_gather(gene_acc, "cells"), axis=0).astype(jnp.bfloat16)
     picked_genes = gene_cast[tile_cols]
     second_terms = jnp.einsum(
         "sik,skr->sir", tiles, picked_genes, preferred_element_type=jnp.float32

time: 302 us -> 569 us (1.88)
  waiting for transfers between devices: 84.7 us -> 451 us
  blocking collectives: 122 us -> 0 us
  other arithmetic: 0.82 us -> 22.8 us
    all_gather x0 -> x1, waiting for transfers between devices: none -> 364 us  [local(): lax.all_gather(gene_acc, 'cells')]
    psum x1 -> x0, blocking collectives: 122 us -> none  [local(): gene_cast = lax.psum(gene_acc, 'cells').astype(jnp.bfloat16)]
    reduce_sum x0 -> x1, other arithmetic: none -> 22 us  [local(): jnp.sum(lax.all_gather(gene_acc, 'cells'), axis=0).astype(jnp.bfloat16)]
  transfers between devices with their start and end apart: 1 -> 2, of which waited for: 1 -> 2; matrix products, arithmetic and copies ran while one was open for 0% -> 0% of each run, Pallas kernels for 0% -> 0%
where the time goes in v1:
time: 569 us
  waiting for transfers between devices  451 us (79%)
  local copies, waits for them, and re-layouts  43.3 us (8%)
  matrix products  36.9 us (6%)
  other arithmetic  22.8 us (4%)
  between operations  14.2 us (2%)
    all_gather x1, waiting for transfers between devices, local(): lax.all_gather(gene_acc, 'cells')  364 us
    reduce_scatter x1, waiting for transfers between devices, local(): lax.psum_scatter(cell_acc.reshape(row_blocks * tile_size, sketch_width),...  87 us
    reduce_sum x1, other arithmetic, local(): jnp.sum(lax.all_gather(gene_acc, 'cells'), axis=0).astype(jnp.bfloat16)  22 us
    dot_general x1, local copies, waits for them, and re-layouts, local(): jnp.einsum('ski,skr->sir', tiles, picked_rows, preferred_element_type=jnp...  12.7 us
    dot_general x1, local copies, waits for them, and re-layouts, local(): jnp.einsum('sik,skr->sir', tiles, picked_genes, preferred_element_type=jn...  12.7 us
  transfers between devices with their start and end apart: 2, of which 2 were waited for; matrix products, arithmetic and copies ran while one was open for 0% of the time, Pallas kernels for 0%

profile of v1, /device:TPU:2, one launch (start us, length us, event | category | flops | bytes accessed | tf_op | source)
XLA Modules:
  0.0 568.9 jit_solution(4233494310680509801)
XLA Ops:
  6.5 0.0 copy-start
  6.5 0.0 all-gather.3.cloned.1.call-start
  7.4 0.8 compare_select_fusion.1
  8.2 6.9 %gather_fusion = bf16[96,128,256]{2,1,0:T(8,128)(2,1)} fusion(bf16[8,128,256]{2,1,0:T(8,128)(2,1)} %bitcast.21, s32[1024]{0:T(1024)S(1)} %pad_clamp_fusion.1), kind=kCustom, calls=%fused_computation | custom fusion | bytes 12583296 | tf_op jit(solution)/shard_map/gather | solution.py:23
  15.1 0.0 copy-done
  15.1 9.2 %convolution_bitcast_fusion.1 = f32[96,128,256]{1,2,0:T(8,128)} fusion(bf16[96,128,256]{2,1,0:T(8,128)(2,1)} %gather_fusion, bf16[96,128,128]{2,1,0:T(8,128)(2,1)S(1)} %copy-done), kind=kOutput, calls=%fused_computation.3 | convolution fusion | flops 805306368 | bytes 22020096 | tf_op jit(solution)/shard_map/ski,skr->sir/dot_general | solution.py:24
  24.3 0.0 copy-start.1
  24.3 12.7 %copy.12 = f32[96,128,256]{2,0,1:T(8,128)} copy(f32[96,128,256]{1,2,0:T(8,128)} %convolution_bitcast_fusion.1) | data formatting | bytes 25165824 | tf_op jit(solution)/shard_map/ski,skr->sir/dot_general | solution.py:24
  37.0 0.0 copy-done.1
  37.0 9.6 %fusion = f32[16,128,256]{2,0,1:T(8,128)} fusion(f32[96,128,256]{2,0,1:T(8,128)} %copy.12, f32[96]{0:T(128)S(1)} %compare_convert_fusion, s32[96]{0:T(128)S(1)} %copy-done.1), kind=kOutput, calls=%fused_computation.5 | convolution fusion | flops 603982848 | bytes 14680832 | tf_op jit(solution)/shard_map/sg,sir->gir/dot_general | solution.py:25
  46.6 0.0 all-gather.3.cloned.1.call-update
  46.6 0.2 reduce-scatter.2.cloned.1.call-start
  46.9 364.4 %all-gather.3.cloned.1.call-done = f32[512,128,256]{2,0,1:T(8,128)} async-done(((f32[16,128,256]{2,0,1:T(8,128)}), f32[512,128,256]{2,0,1:T(8,128)}) %all-gather.3.cloned.1.call-update) | async-done | bytes 67108880 | tf_op jit(solution)/shard_map/all_gather | solution.py:26
  411.3 22.0 %reduce_sum.9 = bf16[16,128,256]{2,0,1:T(8,128)(2,1)} reduce(f32[32,16,128,256]{3,1,0,2:T(8,128)} %bitcast.5, f32[]{:T(128)} %constant.2.clone.1), dimensions={0}, to_apply=%region_0.0 | reduce | flops 16252928 | bytes 68157440 | tf_op jit(solution)/shard_map/reduce_sum | solution.py:26
  433.3 2.5 copy.20
  435.8 7.1 %gather_fusion.1 = bf16[96,128,256]{2,1,0:T(8,128)(2,1)} fusion(bf16[16,128,256]{2,1,0:T(8,128)(2,1)} %copy.20, s32[1024]{0:T(1024)S(1)} %pad_clamp_fusion), kind=kCustom, calls=%fused_computation.1 | custom fusion | bytes 12583296 | tf_op jit(solution)/shard_map/gather | solution.py:27
  442.9 9.2 %convolution_bitcast_fusion = f32[96,128,256]{1,2,0:T(8,128)} fusion(bf16[96,128,256]{2,1,0:T(8,128)(2,1)} %gather_fusion.1, bf16[96,128,128]{2,1,0:T(8,128)(2,1)S(1)} %copy-done), kind=kOutput, calls=%fused_computation.2 | convolution fusion | flops 805306368 | bytes 22020096 | tf_op jit(solution)/shard_map/sik,skr->sir/dot_general | solution.py:28
  452.1 0.0 copy-start.2
  452.1 12.7 %copy.15 = f32[96,128,256]{2,0,1:T(8,128)} copy(f32[96,128,256]{1,2,0:T(8,128)} %convolution_bitcast_fusion) | data formatting | bytes 25165824 | tf_op jit(solution)/shard_map/sik,skr->sir/dot_general | solution.py:28
  464.8 0.0 copy-done.2
  464.8 8.9 %fusion.3 = f32[8,128,256]{2,0,1:T(8,128)S(1)} fusion(f32[96,128,256]{2,0,1:T(8,128)} %copy.15, f32[96]{0:T(128)S(1)} %compare_convert_fusion, s32[96]{0:T(128)S(1)} %copy-done.2), kind=kOutput, calls=%fused_computation.11 | convolution fusion | flops 301991424 | bytes 13632256 | tf_op jit(solution)/shard_map/sb,sir->bir/dot_general | solution.py:31
  473.7 1.3 copy.16
  475.0 0.0 reduce-scatter.2.cloned.1.call-update
  475.1 87.0 %reduce-scatter.2.cloned.1.call-done = f32[64,256]{1,0:T(8,128)} async-done(((f32[1024,256]{1,0:T(8,128)}), f32[64,256]{1,0:T(8,128)}) %reduce-scatter.2.cloned.1.call-update) | async-done | bytes 65552 | tf_op jit(solution)/shard_map/reduce_scatter | solution.py:32
  (4 shorter events, 0.0 us)
Async XLA Ops:
  6.5 8.6 %copy-start = (bf16[96,128,128]{2,1,0:T(8,128)(2,1)S(1)}, bf16[96,128,128]{2,1,0:T(8,128)(2,1)}, u32[]{:S(2)}) copy-start(bf16[96,128,128]{2,1,0:T(8,128)(2,1)} %param.6) | copy-start | bytes 9437188
  6.5 404.8 %all-gather.3.cloned.1.call-start = ((), (), s32[]{:S(2)}) async-start(), calls=%async_computation.2 | async-start | bytes 69206016 | tf_op jit(solution)/shard_map/all_gather | solution.py:26
  24.3 12.7 %copy-start.1 = (s32[96]{0:T(128)S(1)}, s32[96]{0:T(128)}, u32[]{:S(2)}) copy-start(s32[96]{0:T(128)} %param.8) | copy-start | bytes 1156
  46.6 515.4 %reduce-scatter.2.cloned.1.call-start = ((), (), s32[]{:S(2)}) async-start(), calls=%async_computation.1 | async-start | bytes 1114112 | tf_op jit(solution)/shard_map/reduce_scatter | solution.py:32
  452.1 12.7 %copy-start.2 = (s32[96]{0:T(128)S(1)}, s32[96]{0:T(128)}, u32[]{:S(2)}) copy-start(s32[96]{0:T(128)} %param.7) | copy-start | bytes 1156
Sparse Core Ops, SparseCore 0:
  46.8 364.5 all-gather.2
  475.2 86.8 reduce-scatter.1
